TPU v7x, 256 devices: a whole 4x4x8 slice. The times are simulated.
256 devices in a mesh: grp: 8 (over y, z_lo), dev: 32 (over x, z_hi, core).
Axes of the slice: x: 4, y: 4, z: 8 (z_hi: 4, z_lo: 2; z = z_hi * 2 + z_lo), core: 2. Of those that a mesh axis runs over, the one named last changes fastest.
Arguments:
- resid: bfloat16 [32768, 1536], P(('grp', 'dev')), may hold values from -1.5 to 1.5
- queries: bfloat16 [32768, 1536], P(('grp', 'dev')), may hold values from -6 to 6
- suffix_kv: bfloat16 [32768, 2, 512], P(('grp', 'dev')), may hold values from -6 to 6
- prefix_kv: bfloat16 [8, 2048, 2, 512], P('grp', 'dev'), may hold values from -6 to 6
- segments: int32 [256, 128], P(('grp', 'dev')), may hold values from 0 to 3, never falling along the last dimension, each value on 1 to 64 neighbouring positions
- o_weight: bfloat16 [1536, 1536], P(('grp', 'dev')), may hold values from -0.15625 to 0.15625
- norm_gain: float32 [1536], replicated, may hold values from 0.25 to 1.75
- router: bfloat16 [1536, 32], replicated, may hold values from -0.15625 to 0.15625
- routes: int32 [32768, 8], P(('grp', 'dev')), may hold values from 0 to 31, all different within a row; in each aligned block of 128 rows (0 to 127, 128 to 255, ...) at most 48 rows name the same one
- w_gate_up: bfloat16 [32, 1536, 1024], P('dev', 'grp'), may hold values from -0.15625 to 0.15625
- w_down: bfloat16 [32, 512, 1536], P('dev', 'grp'), may hold values from -0.25 to 0.25
Outputs:
- layer_out: bfloat16 [32768, 1536], P(('grp', 'dev'))
Inputs may be any that keep to these rules, and one draw needn't show every extreme that they name: At most 48 of one device's routes name one expert.
All inputs are finite; a program needn't handle non-finite values.
Results may differ from a plain program's by a relative error of at most 0.012.
Values may be sent and summed in bfloat16 or wider, within the bound.
A program may use at most 128 MiB of HBM per device.

v0:
```python
import jax
import jax.numpy as jnp
from jax import lax
from jax.sharding import PartitionSpec as P

D = 1536
HEADS = 24
KVH = 8
HDIM = 64
FFE = 512
TOPK = 8
EXPERTS = 32
ATT = 1536
CAP = 48


def per_device(
    resid,
    queries,
    suffix_kv,
    prefix_kv,
    segments,
    o_weight,
    norm_gain,
    router,
    routes,
    w_gate_up,
    w_down,
):
    tok_rows = resid.shape[0]
    ratio = HEADS // KVH
    scale = 1.0 / HDIM**0.5
    query_heads = queries.reshape(tok_rows, KVH, ratio, HDIM)

    def update(carry, keys, values, mask):
        running, totals, accum = carry
        count = keys.shape[0]
        scores = (
            jnp.einsum(
                "tgrd,ngd->grtn",
                query_heads,
                keys.reshape(count, KVH, HDIM),
                preferred_element_type=jnp.float32,
            )
            * scale
        )
        if mask is not None:
            scores = jnp.where(mask[None, None], scores, jnp.float32(-1e30))
        newmax = jnp.maximum(running, jnp.max(scores, axis=-1))
        factor = jnp.exp(running - newmax)
        weights = jnp.exp(scores - newmax[..., None])
        totals = totals * factor + jnp.sum(weights, axis=-1)
        accum = accum * factor[..., None] + jnp.einsum(
            "grtn,ngd->grtd",
            weights.astype(jnp.bfloat16),
            values.reshape(count, KVH, HDIM),
            preferred_element_type=jnp.float32,
        )
        return (newmax, totals, accum)

    initial = (
        jnp.full((KVH, ratio, tok_rows), -1e30, jnp.float32),
        jnp.zeros((KVH, ratio, tok_rows), jnp.float32),
        jnp.zeros((KVH, ratio, tok_rows, HDIM), jnp.float32),
    )
    piece = lax.all_gather(prefix_kv[0], "dev", axis=0, tiled=True)
    carry = update(initial, piece[:, 0], piece[:, 1], None)
    seg_row = segments[0]
    positions = jnp.arange(tok_rows, dtype=jnp.int32)
    local_mask = (seg_row[:, None] == seg_row[None, :]) & (positions[None, :] <= positions[:, None])
    running, totals, accum = update(carry, suffix_kv[:, 0], suffix_kv[:, 1], local_mask)
    attended = (
        (accum / totals[..., None])
        .transpose(2, 0, 1, 3)
        .reshape(tok_rows, ATT)
        .astype(jnp.bfloat16)
    )
    projected = jnp.dot(
        attended,
        lax.all_gather(o_weight, ("grp", "dev"), axis=0, tiled=True),
        preferred_element_type=jnp.float32,
    )
    hidden = resid.astype(jnp.float32) + projected
    inverse = lax.rsqrt(jnp.mean(hidden * hidden, axis=-1, keepdims=True) + 1e-06)
    normed = (hidden * inverse * norm_gain).astype(jnp.bfloat16)
    logits = jnp.dot(normed, router, preferred_element_type=jnp.float32)
    expert_ids = jnp.arange(EXPERTS, dtype=jnp.int32)
    onehot = routes[:, :, None] == expert_ids[None, None, :]
    chosen = jnp.sum(jnp.where(onehot, logits[:, None, :], 0.0), axis=-1)
    sig = jax.nn.sigmoid(chosen)
    gates = (sig / jnp.sum(sig, axis=-1, keepdims=True)).astype(jnp.bfloat16)
    flat = onehot.reshape(tok_rows * TOPK, EXPERTS).astype(jnp.int32)
    before = jnp.cumsum(flat, axis=0) - flat
    slot = jnp.sum(before * flat, axis=-1).reshape(tok_rows, TOPK)
    place = routes * CAP + slot
    slot_ids = jnp.arange(EXPERTS * CAP, dtype=jnp.int32)
    hits = place[None, :, :] == slot_ids[:, None, None]
    table = jnp.sum(hits.astype(jnp.float32), axis=-1).astype(jnp.bfloat16)
    dispatch = jnp.dot(table, normed, preferred_element_type=jnp.float32).astype(jnp.bfloat16)
    dispatch = dispatch.reshape(EXPERTS, CAP, D)
    slot_count = dispatch.shape[1]
    received = lax.all_to_all(dispatch, "dev", split_axis=0, concat_axis=1, tiled=True)
    sliced = received
    gate_up = jnp.einsum(
        "erd,edf->erf",
        sliced,
        lax.all_gather(w_gate_up, "grp", axis=1, tiled=True),
        preferred_element_type=jnp.float32,
    )
    act = (jax.nn.silu(gate_up[..., :FFE]) * gate_up[..., FFE:]).astype(jnp.bfloat16)
    sliced = act
    expert_out = jnp.einsum(
        "erf,efd->erd",
        sliced,
        lax.all_gather(w_down, "grp", axis=1, tiled=True),
        preferred_element_type=jnp.float32,
    ).astype(jnp.bfloat16)
    returned = lax.all_to_all(expert_out, "dev", split_axis=1, concat_axis=0, tiled=True)
    returned = returned.reshape(EXPERTS * slot_count, D)
    back_hits = place[:, :, None] == slot_ids[None, None, :]
    ctable = jnp.sum(
        jnp.where(back_hits, gates[:, :, None].astype(jnp.float32), 0.0), axis=1
    ).astype(jnp.bfloat16)
    mixed = jnp.dot(ctable, returned, preferred_element_type=jnp.float32)
    return (hidden + mixed).astype(jnp.bfloat16)


def solution(mesh):
    return jax.shard_map(
        per_device,
        mesh=mesh,
        in_specs=(
            P(("grp", "dev"), None),
            P(("grp", "dev"), None),
            P(("grp", "dev"), None, None),
            P("grp", "dev", None, None),
            P(("grp", "dev"), None),
            P(("grp", "dev"), None),
            P(),
            P(),
            P(("grp", "dev"), None),
            P("dev", "grp", None),
            P("dev", "grp", None),
        ),
        out_specs=P(("grp", "dev"), None),
        check_vma=False,
    )
```

profile of v0, /device:TPU:70, one launch (start us, length us, event | category | flops | bytes accessed | tf_op | source)
XLA Modules:
  0.0 969.9 jit_solution(531432880128900151)
XLA Ops:
  7.4 0.7 all-gather.11.cloned.1.call-update
  8.8 0.8 copy.98
  9.8 1.2 copy.92
  11.0 1.5 fusion.54
  12.9 9.0 reduce-window.6
  22.6 0.7 multiply_add_fusion
  23.3 8.0 convert_reduce_fusion
  31.4 1.6 fusion.55
  33.0 38.9 %all-gather.11.cloned.1.call-done = bf16[1,2048,2,512]{3,2,0,1:T(2,128)(2,1)} async-done(((bf16[1,64,2,512]{3,2,0,1:T(2,128)(2,1)}), bf16[1,2048,2,512]{3,2,0,1:T(2,128)(2,1)}) %all-gather.11.cloned.1.call-update) | async-done | bytes 4194320 | tf_op jit(solution)/shard_map/all_gather | solution.py:66
  71.9 9.9 %fusion.53 = (bf16[2048,1,512]{2,1,0:T(2,128)(2,1)}, bf16[2048,1,512]{2,1,0:T(2,128)(2,1)}) fusion(bf16[2048,2,512]{2,1,0:T(2,128)(2,1)} %bitcast.137), kind=kLoop, calls=%fused_computation.72 | loop fusion | bytes 8388608 | tf_op jit(solution)/shard_map/slice | solution.py:67
  81.9 10.6 %copy.93 = bf16[2048,1,512]{0,2,1:T(8,128)(2,1)} copy(bf16[2048,1,512]{2,1,0:T(2,128)(2,1)} %get-tuple-element.8) | data formatting | bytes 4194304 | tf_op jit(solution)/shard_map/slice | solution.py:67
  92.4 9.0 copy.91
  101.4 10.1 %bitcast_reduce_fusion = (f32[8,3,128]{2,1,0:T(4,128)S(1)}, f32[8,2048,128,3]{2,1,3,0:T(8,128)}) fusion(bf16[2048,8,64,1]{0,2,3,1:T(8,128)(2,1)S(1)} %bitcast.138, bf16[128,8,3,64]{0,3,2,1:T(8,128)(2,1)S(1)} %bitcast.142), kind=kOutput, calls=%fused_computation.1 | convolution fusion | flops 817886208 | bytes 27668480 | tf_op jit(solution)/shard_map/tgrd,ngd->grtn/dot_general | solution.py:39
  111.9 10.6 %fusion.1 = f32[8,3,128]{2,1,0:T(4,128)S(1)} fusion(f32[8,2048,128,3]{2,1,3,0:T(8,128)} %get-tuple-element.17, f32[8,3,128]{2,1,0:T(4,128)S(1)} %get-tuple-element.13), kind=kLoop, calls=%fused_computation.3 | loop fusion | flops 18871296 | bytes 25190400 | tf_op jit(solution)/shard_map/reduce_sum | solution.py:52
  122.5 10.5 %fusion.30 = f32[128,8,3,64]{0,3,2,1:T(8,128)S(1)} fusion(bf16[2048,8,64,1]{0,2,3,1:T(8,128)(2,1)S(1)} %bitcast.140, f32[8,2048,128,3]{2,1,3,0:T(8,128)} %get-tuple-element.17, f32[8,3,128]{2,1,0:T(4,128)S(1)} %get-tuple-element.13, f32[128,8,3]{0,2,1:T(4,128)S(1)} %get-tuple-element.6, f32[128,8,3]{0,2,1:T(4,128)S(1)} %get-tuple-element.11), kind=kOutput, calls=%fused_computation.34 | convolution fusion | flops 824573952 | bytes 28086272 | tf_op jit(solution)/shard_map/grtn,ngd->grtd/dot_general | solution.py:53
  133.5 351.7 %all-gather.13.cloned.1.call-done = bf16[256,6,1536]{2,1,0:T(8,128)(2,1)} async-done(((bf16[1,6,1536]{2,1,0:T(8,128)(2,1)}), bf16[256,6,1536]{2,1,0:T(8,128)(2,1)}) %all-gather.13.cloned.1.call-update) | async-done | bytes 4718608 | tf_op jit(solution)/shard_map/all_gather | solution.py:80
  485.1 8.4 reshape.176
  493.5 3.2 multiply_reduce_fusion
  496.8 3.6 convolution_convert_fusion.1
  500.4 14.8 %all-to-all-start = ((bf16[32,48,1536]{2,1,0:T(8,128)(2,1)}), bf16[32,48,1536]{2,1,0:T(8,128)(2,1)}, u32[]{:S(2)}, u32[]{:S(2)}) async-start(bf16[32,48,1536]{2,1,0:T(8,128)(2,1)} %bitcast.135), calls=%async_computation | async-start | bytes 9437184 | tf_op jit(solution)/shard_map/all_to_all | solution.py:102
  516.4 160.2 %all-gather.7.cloned.1.call-done = bf16[1,1536,1024]{2,1,0:T(8,128)(2,1)} async-done(((bf16[1,192,1024]{2,1,0:T(8,128)(2,1)}), bf16[1,1536,1024]{2,1,0:T(8,128)(2,1)}) %all-gather.7.cloned.1.call-update) | async-done | bytes 3145744 | tf_op jit(solution)/shard_map/all_gather | solution.py:107
  676.6 9.8 %convolution_bitcast_fusion = f32[1,1536,1024]{2,1,0:T(8,128)} fusion(bf16[1536,1536]{1,0:T(8,128)(2,1)} %bitcast.29, bf16[1,1536,1024]{2,1,0:T(8,128)(2,1)} %all-gather.7.cloned.1.call-done), kind=kOutput, calls=%fused_computation.16 | convolution fusion | flops 4831838208 | bytes 14155776 | tf_op jit(solution)/shard_map/erd,edf->erf/dot_general | solution.py:104
  686.4 37.1 %all-gather.9.cloned.1.call-done = bf16[1,512,1536]{2,1,0:T(8,128)(2,1)} async-done(((bf16[1,64,1536]{2,1,0:T(8,128)(2,1)}), bf16[1,512,1536]{2,1,0:T(8,128)(2,1)}) %all-gather.9.cloned.1.call-update) | async-done | bytes 1572880 | tf_op jit(solution)/shard_map/all_gather | solution.py:115
  723.5 6.0 fusion.5
  729.5 52.2 %copy.124 = bf16[1,1536,1536]{2,0,1:T(2,128)(2,1)} copy(bf16[1,1536,1536]{2,1,0:T(8,128)(2,1)S(1)} %fusion.5) | data formatting | bytes 9437184 | tf_op jit(solution)/shard_map/convert_element_type | solution.py:117
  782.2 32.0 %reduce = bf16[1536,1536]{1,0:T(8,128)(2,1)} reduce(bf16[1536,1,1536]{2,1,0:T(2,128)(2,1)} %bitcast.136, bf16[]{:T(256)} %broadcast.126), dimensions={1}, to_apply=%bitcast.134.reduce_sub_computation | reduce | bytes 9437186
  814.2 8.2 reshape.181
  822.3 9.3 all-to-all-start.1
  832.2 2.1 select_reduce_fusion
  834.3 102.8 %all-to-all-done.1 = bf16[32,2,36864]{2,1,0:T(2,128)(2,1)} async-done(((bf16[32,2,36864]{2,1,0:T(2,128)(2,1)}), bf16[32,2,36864]{2,1,0:T(2,128)(2,1)}, u32[]{:S(2)}, u32[]{:S(2)}) %all-to-all-start.1) | async-done | bytes 4718624 | tf_op jit(solution)/shard_map/all_to_all | solution.py:118
  937.1 20.2 %reshape.182 = bf16[1536,1,1536]{2,1,0:T(2,128)(2,1)} reshape(bf16[32,2,36864]{2,1,0:T(2,128)(2,1)} %all-to-all-done.1) | data formatting | bytes 9437184
  957.3 5.2 fusion.14
  (49 shorter events, 5.0 us)
Async XLA Ops:
  7.4 824.4 %copy-start = (bf16[1536,32]{0,1:T(8,128)(2,1)S(1)}, bf16[1536,32]{0,1:T(8,128)(2,1)}, u32[]{:S(2)}) copy-start(bf16[1536,32]{0,1:T(8,128)(2,1)} %param.18) | copy-start | bytes 294916
  7.4 24.0 %copy-start.6 = (s32[1,128]{1,0:T(1,128)S(1)}, s32[1,128]{1,0:T(1,128)}, u32[]{:S(2)}) copy-start(s32[1,128]{1,0:T(1,128)} %param.15) | copy-start | bytes 1540
  7.4 64.5 %all-gather.11.cloned.1.call-start = ((), (), s32[]{:S(2)}) async-start(), calls=%async_computation.4 | async-start | bytes 4325376 | tf_op jit(solution)/shard_map/all_gather | solution.py:66
  8.1 477.0 %all-gather.13.cloned.1.call-start = ((), (), s32[]{:S(2)}) async-start(), calls=%async_computation.5 | async-start | bytes 6316032 | tf_op jit(solution)/shard_map/all_gather | solution.py:80
  101.4 10.2 %copy-start.2 = (f32[8,3,128,128]{2,3,1,0:T(8,128)S(1)}, f32[8,3,128,128]{2,3,1,0:T(8,128)}, u32[]{:S(2)}) copy-start(f32[8,3,128,128]{2,3,1,0:T(8,128)} %get-tuple-element.15) | copy-start | bytes 4718596
  111.9 10.7 %copy-start.1 = (bf16[2048,1,512]{0,2,1:T(8,128)(2,1)S(1)}, bf16[2048,1,512]{0,2,1:T(8,128)(2,1)}, u32[]{:S(2)}) copy-start(bf16[2048,1,512]{0,2,1:T(8,128)(2,1)} %copy.93) | copy-start | bytes 6291460
  133.4 360.1 %copy-start.3 = (bf16[128,1536]{1,0:T(8,128)(2,1)S(1)}, bf16[128,1536]{1,0:T(8,128)(2,1)}, u32[]{:S(2)}) copy-start(bf16[128,1536]{1,0:T(8,128)(2,1)} %param.11) | copy-start | bytes 1179652
  493.5 3.3 copy-start.5
  500.4 176.2 %all-to-all-start = ((bf16[32,48,1536]{2,1,0:T(8,128)(2,1)}), bf16[32,48,1536]{2,1,0:T(8,128)(2,1)}, u32[]{:S(2)}, u32[]{:S(2)}) async-start(bf16[32,48,1536]{2,1,0:T(8,128)(2,1)} %bitcast.135), calls=%async_computation | async-start | bytes 9437184 | tf_op jit(solution)/shard_map/all_to_all | solution.py:102
  515.2 161.4 %all-gather.7.cloned.1.call-start = ((), (), s32[]{:S(2)}) async-start(), calls=%async_computation.2 | async-start | bytes 3538944 | tf_op jit(solution)/shard_map/all_gather | solution.py:107
  515.8 207.7 %all-gather.9.cloned.1.call-start = ((), (), s32[]{:S(2)}) async-start(), calls=%async_computation.3 | async-start | bytes 1769472 | tf_op jit(solution)/shard_map/all_gather | solution.py:115
  822.3 9.7 copy-start.4
  822.3 114.7 %all-to-all-start.1 = ((bf16[32,2,36864]{2,1,0:T(2,128)(2,1)}), bf16[32,2,36864]{2,1,0:T(2,128)(2,1)}, u32[]{:S(2)}, u32[]{:S(2)}) async-start(bf16[32,2,36864]{2,1,0:T(2,128)(2,1)} %reshape.181), calls=%async_computation.1 | async-start | bytes 9437184 | tf_op jit(solution)/shard_map/all_to_all | solution.py:118
Sparse Core Ops, SparseCore 0:
  10.7 61.1 all-gather.10
  73.8 411.2 all-gather.12
Sparse Core Ops, SparseCore 1:
  517.5 159.1 all-gather.6
  678.3 45.2 all-gather.8
where the time goes:
time: 976 us; the launch traced here: 970 us
  waiting for transfers between devices  693 us (71%)
  local copies, waits for them, and re-layouts  124 us (13%)
  other arithmetic  63.1 us (6%)
  matrix products  50.7 us (5%)
  starting transfers between devices  24.3 us (2%)
  between operations  15.1 us (2%)
    all_gather x1, waiting for transfers between devices, per_device(): lax.all_gather(o_weight, ('grp', 'dev'), axis=0, tiled=True)  352 us
    all_gather x1, waiting for transfers between devices, per_device(): lax.all_gather(w_gate_up, 'grp', axis=1, tiled=True)  160 us
    all_to_all x1, waiting for transfers between devices, per_device(): lax.all_to_all(expert_out, 'dev', split_axis=1, concat_axis=0, tiled=True)  103 us
    convert_element_type x1, local copies, waits for them, and re-layouts, per_device(): expert_out = jnp.einsum('erf,efd->erd', sliced, lax.all_gather(w_down, 'g...  52.2 us
    unnamed x20, local copies, waits for them, and re-layouts  39.3 us
    all_gather x1, waiting for transfers between devices, per_device(): piece = lax.all_gather(prefix_kv[0], 'dev', axis=0, tiled=True)  38.9 us
    all_gather x1, waiting for transfers between devices, per_device(): lax.all_gather(w_down, 'grp', axis=1, tiled=True)  37.1 us
    unnamed x1, other arithmetic  32 us
  transfers between devices with their start and end apart: 6, of which 5 were waited for; matrix products, arithmetic and copies ran while one was open for 10% of the time, Pallas kernels for 0%

commit v1 on v0

v1 whole, which is shorter than its diff:
```python
import functools

import jax
import jax.numpy as jnp
import numpy as np
from jax import lax
from jax.experimental import pallas as pl
from jax.experimental.pallas import tpu as pltpu
from jax.sharding import PartitionSpec as P

D = 1536
KVH = 8
FFE = 512
CAP = 48
EXPERTS = 32
TOK = 128
ROWS = 144
BF = jnp.bfloat16
F32 = jnp.float32
MESH = pl.DeviceIdType.MESH


def spread_matrix():
    out = np.zeros((384, 512), np.float32)
    for q in range(512):
        i, z, x, c = q % 8, (q // 8) % 8, (q // 64) % 4, q // 256
        if i < 6:
            out[((z % 2) * 32 + x * 8 + (z // 2) * 2 + c) * 6 + i, q] = 1.0
    return out


class Copies:
    def __init__(self, send, recv):
        self.send, self.recv, self.sends, self.recvs, self.open = send, recv, 0, 0, []

    def slot(self):
        self.recvs += 1
        return self.recvs - 1

    def start(self, src, dst, slot, device, again=None):
        copy = pltpu.make_async_remote_copy(
            src_ref=src,
            dst_ref=dst,
            send_sem=self.send.at[self.sends],
            recv_sem=self.recv.at[slot],
            device_id=device,
            device_id_type=MESH,
        )
        self.open.append((self.sends, again or (lambda: src)))
        self.sends += 1
        copy.start()

    def arrived(self, ref, slot):
        pltpu.make_async_copy(ref, ref, self.recv.at[slot]).wait()

    def drain(self):
        for index, source in self.open:
            ref = source()
            pltpu.make_async_copy(ref, ref, self.send.at[index]).wait()


def kernel(
    resid,
    queries,
    suffix,
    kv_own,
    seg_row,
    seg_col,
    o_own,
    spread,
    gain,
    router_t,
    routes_t,
    w1_own,
    w2_own,
    out,
    KV,
    O,
    W1,
    W2,
    XG,
    QH,
    OH,
    AP,
    MK,
    HID,
    XD,
    Y,
    CM,
    PF,
    CS,
    CR,
    S1S,
    S1R,
    S2S,
    S2R,
    ZS,
    ZR,
    send_sem,
    recv_sem,
    local_sem,
):
    grp, dev = lax.axis_index("grp"), lax.axis_index("dev")
    y, zl = lax.div(grp, 2), lax.rem(grp, 2)
    x, zh, c = lax.div(dev, 8), lax.rem(lax.div(dev, 2), 4), lax.rem(dev, 2)

    def at(x_=x, y_=y, zh_=zh, zl_=zl, c_=c):
        return (y_ * 2 + zl_, x_ * 8 + zh_ * 2 + c_)

    def up(v, k=1):
        return lax.rem(v + k, 4)

    right, left, partner = at(x_=up(x)), at(x_=up(x, 3)), at(c_=1 - c)
    sides = (right, left)
    y_sides = (at(y_=up(y)), at(y_=up(y, 3)))
    beside = at(zl_=1 - zl)

    barrier = pltpu.get_barrier_semaphore()
    friends = [right, left, partner, y_sides[0], y_sides[1], at(y_=up(y, 2)), beside]
    for k in (1, 2, 3):
        friends += [at(zh_=up(zh, k)), at(zh_=up(zh, k), zl_=1 - zl)]
    for friend in friends:
        pl.semaphore_signal(barrier, inc=1, device_id=friend, device_id_type=MESH)
    pl.semaphore_wait(barrier, len(friends))

    cp = Copies(send_sem, recv_sem)

    def kv_slot(x_, zh_, c_=c):
        return x_ * 8 + zh_ * 2 + c_

    kv_z = [None] + [cp.slot() for _ in range(3)]
    kv_x = [[cp.slot() for _ in range(2)] for _ in range(4)]
    kv_half = [[cp.slot() for _ in range(2)] for _ in range(4)]
    kv_p = [[cp.slot() for _ in range(4)] for _ in range(4)]
    o_z = [[cp.slot() for _ in range(2)] for _ in range(4)]
    o_y = [None] + [cp.slot() for _ in range(3)]
    o_x = [cp.slot() for _ in range(2)]
    o_half = [cp.slot() for _ in range(2)]
    o_p = [cp.slot() for _ in range(4)]
    w_z = [[[cp.slot() for _ in range(3)] for _ in range(2)] for _ in range(2)]
    w_y = [[[cp.slot() for _ in range(3)] for _ in range(2)] for _ in range(2)]
    w_half = [[[cp.slot() for _ in range(3)] for _ in range(2)] for _ in range(2)]
    t_zl = cp.slot()
    t_x = [[cp.slot() for _ in range(2)] for _ in range(2)]
    t_half = [[cp.slot() for _ in range(2)] for _ in range(2)]
    t_p = [[cp.slot() for _ in range(4)] for _ in range(2)]
    s_c = cp.recvs
    for _ in range(8):
        cp.slot()
    s_1 = [[cp.slot() for _ in range(2)] for _ in range(2)]
    s_2 = [[cp.slot() for _ in range(2)] for _ in range(2)]
    s_z = cp.slot()

    mine = KV.at[kv_slot(x, zh)]
    local_kv = pltpu.make_async_copy(kv_own, mine, local_sem.at[0])
    local_kv.start()
    for k in (1, 2, 3):
        cp.start(kv_own, mine, kv_z[k], at(zh_=up(zh, k)))
    for i in range(2):
        cp.start(kv_own, mine, kv_x[0][i], sides[i])
    cp.start(kv_own, mine, kv_p[0][0], partner)

    my_z = zh * 2 + zl
    o_mine = O.at[y, c, x, my_z]
    local_o = pltpu.make_async_copy(o_own, o_mine, local_sem.at[1])
    local_o.start()
    for k in range(4):
        for j in range(2):
            if k or j:
                cp.start(o_own, o_mine, o_z[k][j], at(zh_=up(zh, k), zl_=zl if j == 0 else 1 - zl))

    pieces = (
        lambda j, y_, z_: W1.at[j, y_, z_, 0],
        lambda j, y_, z_: W1.at[j, y_, z_, 1],
        lambda j, y_, z_: W2.at[j, y_, z_],
    )
    own_pieces = (w1_own.at[0], w1_own.at[1], w2_own)
    w_target = lax.div(zh, 2)
    w_started = []

    def w_start(n):
        for j in range(2):
            for z_ in range(2):

                @pl.when((lax.rem(zh, 2) == j) & (zl == z_))
                def _():
                    for k in range(4):
                        sem = send_sem.at[cp.sends + k]
                        copy = pltpu.make_async_remote_copy(
                            src_ref=own_pieces[n],
                            dst_ref=pieces[n](j, y, z_),
                            send_sem=sem,
                            recv_sem=recv_sem.at[w_z[j][z_][n]],
                            device_id=at(zh_=up(zh, k), zl_=w_target),
                            device_id_type=MESH,
                        )
                        if k:
                            copy.start()
                        else:

                            @pl.when(w_target != zl)
                            def _():
                                copy.start()

                            @pl.when(w_target == zl)
                            def _():
                                pltpu.make_async_copy(
                                    own_pieces[n], pieces[n](j, y, z_), recv_sem.at[w_z[j][z_][n]]
                                ).start()

        w_started.append((n, cp.sends))
        cp.sends += 4

    def w_drain():
        for n, first in w_started:
            for k in range(4):
                copy = pltpu.make_async_remote_copy(
                    src_ref=own_pieces[n],
                    dst_ref=pieces[n](0, y, 0),
                    send_sem=send_sem.at[first + k],
                    recv_sem=recv_sem.at[w_z[0][0][n]],
                    device_id=at(zh_=up(zh, k), zl_=w_target),
                    device_id_type=MESH,
                )
                if k:
                    copy.wait_send()
                else:

                    @pl.when(w_target != zl)
                    def _():
                        copy.wait_send()

    def w_along_y(n):
        for j in range(2):
            for z_ in range(2):
                cp.arrived(pieces[n](j, y, z_), w_z[j][z_][n])
            both = pieces[n](j, y, slice(None))
            for i in range(2):
                cp.start(both, both, w_y[j][i][n], y_sides[i])

    def w_forward(n):
        for j in range(2):
            for i in range(2):
                origin = up(y, 3) if i == 0 else up(y)
                cp.arrived(pieces[n](j, origin, slice(None)), w_y[j][i][n])
                half = pieces[n](j, origin, i)
                cp.start(half, half, w_half[j][i][n], y_sides[i])

    def w_finish(n):
        for j in range(2):
            for i in range(2):
                cp.arrived(pieces[n](j, up(y, 2), i), w_half[j][i][n])

    for n in range(3):
        w_start(n)

    lane = lax.broadcasted_iota(jnp.int32, (TOK, 128), 1)
    low = lane < 64
    for p in range(4):
        tiles = [queries[:, p * 384 + 128 * i : p * 384 + 128 * (i + 1)].astype(F32) * 0.125 for i in range(3)]
        turned = [pltpu.roll(t, 64, 1) for t in (tiles[0], tiles[2])]
        heads = (
            jnp.where(low, tiles[0], 0.0),
            jnp.where(low, turned[0], 0.0),
            jnp.where(low, tiles[1], 0.0),
            jnp.where(low, 0.0, tiles[1]),
            jnp.where(low, 0.0, turned[1]),
            jnp.where(low, 0.0, tiles[2]),
        )
        for h in range(6):
            QH[2 * p + h // 3, (h % 3) * 128 : (h % 3 + 1) * 128, :] = heads[h].astype(BF)
    row = lax.broadcasted_iota(jnp.int32, (TOK, TOK), 0)
    col = lax.broadcasted_iota(jnp.int32, (TOK, TOK), 1)
    allowed = (seg_row[...] == seg_col[...]) & (col <= row)
    bias = jnp.where(allowed, 0.0, -1e30)
    for i in range(3):
        MK[i * 128 : (i + 1) * 128, :] = bias

    for k in (1, 2, 3):
        piece = KV.at[kv_slot(x, up(zh, 4 - k))]
        cp.arrived(piece, kv_z[k])
        for i in range(2):
            cp.start(piece, piece, kv_x[k][i], sides[i])
        cp.start(piece, piece, kv_p[k][0], partner)
    for k in range(4):
        for i in range(2):
            slot = kv_slot(up(x, 3) if i == 0 else up(x), up(zh, 4 - k))
            piece = KV.at[slot]
            cp.arrived(piece, kv_x[k][i])
            half = KV.at[slot, 32 * i : 32 * (i + 1)]
            cp.start(half, half, kv_half[k][i], sides[i])
            cp.start(piece, piece, kv_p[k][1 + i], partner)
    local_o.wait()
    for k in range(4):
        for j in range(2):
            if k or j:
                zz = up(zh, 4 - k) * 2 + (zl if j == 0 else 1 - zl)
                cp.arrived(O.at[y, c, x, zz], o_z[k][j])
    for k in (1, 2, 3):
        cp.start(O.at[y, c, x], O.at[y, c, x], o_y[k], at(y_=up(y, k)))
    for k in range(4):
        slot = kv_slot(up(x, 2), up(zh, 4 - k))
        for i in range(2):
            cp.arrived(KV.at[slot, 32 * i : 32 * (i + 1)], kv_half[k][i])
        cp.start(KV.at[slot], KV.at[slot], kv_p[k][3], partner)
    for k in (1, 2, 3):
        cp.arrived(O.at[up(y, 4 - k), c, x], o_y[k])
    for i in range(2):
        cp.start(O.at[:, c, x], O.at[:, c, x], o_x[i], sides[i])
    cp.start(O.at[:, c, x], O.at[:, c, x], o_p[0], partner)
    for k in range(4):
        for i, from_x in enumerate((x, up(x, 3), up(x), up(x, 2))):
            cp.arrived(KV.at[kv_slot(from_x, up(zh, 4 - k), 1 - c)], kv_p[k][i])
    local_kv.wait()

    nt = (((1,), (1,)), ((), ()))

    def attend(h):
        p = lax.div(h, 2)
        k_cols = pl.ds(pl.multiple_of(p * 128, 128), 128)
        v_cols = pl.ds(pl.multiple_of(512 + p * 128, 128), 128)
        q = QH[h]
        s1 = lax.dot_general(q, KV[:, :, k_cols].reshape(2048, 128), nt, preferred_element_type=F32)
        s2 = lax.dot_general(q, suffix[:, k_cols], nt, preferred_element_type=F32) + MK[...]
        top = jnp.maximum(jnp.max(s1, axis=1, keepdims=True), jnp.max(s2, axis=1, keepdims=True))
        p1, p2 = jnp.exp(s1 - top), jnp.exp(s2 - top)
        total = jnp.sum(p1, axis=1, keepdims=True) + jnp.sum(p2, axis=1, keepdims=True)
        acc = jnp.dot(p1.astype(BF), KV[:, :, v_cols].reshape(2048, 128), preferred_element_type=F32)
        acc += jnp.dot(p2.astype(BF), suffix[:, v_cols], preferred_element_type=F32)
        OH[h] = acc / total

    @pl.loop(0, 2)
    def _(h):
        attend(h)

    w_along_y(0)

    @pl.loop(2, 5)
    def _(h):
        attend(h)

    w_along_y(1)
    for i in range(2):
        origin = up(x, 3) if i == 0 else up(x)
        cp.arrived(O.at[:, c, origin], o_x[i])
        half = O.at[pl.ds(2 * i, 2), c, origin]
        cp.start(half, half, o_half[i], sides[i])
        cp.start(O.at[:, c, origin], O.at[:, c, origin], o_p[1 + i], partner)

    @pl.loop(5, 8)
    def _(h):
        attend(h)

    for p in range(4):
        a = [OH[2 * p + h // 3, (h % 3) * 128 : (h % 3 + 1) * 128, :] for h in range(6)]
        tiles = (
            jnp.where(low, a[0], pltpu.roll(a[1], 64, 1)),
            jnp.where(low, a[2], a[3]),
            jnp.where(low, pltpu.roll(a[4], 64, 1), a[5]),
        )
        att = jnp.concatenate([t.astype(BF) for t in tiles], axis=1)
        AP[p] = jnp.dot(att, spread[...], preferred_element_type=F32).astype(BF)

    far = up(x, 2)
    for i in range(2):
        cp.arrived(O.at[pl.ds(2 * i, 2), c, far], o_half[i])
    cp.start(O.at[:, c, far], O.at[:, c, far], o_p[3], partner)
    w_along_y(2)
    for i, from_x in enumerate((x, up(x, 3), up(x), far)):
        cp.arrived(O.at[:, 1 - c, from_x], o_p[i])

    total = resid[...].astype(F32)
    for p in range(4):
        total += jnp.dot(AP[p], O[p].reshape(512, D), preferred_element_type=F32)
    HID[...] = total
    scale = lax.rsqrt(jnp.mean(total * total, axis=1, keepdims=True) + 1e-06)
    normed = (total * scale * gain[...]).astype(BF)
    logits = lax.dot_general(router_t[...], normed, nt, preferred_element_type=F32)
    expert = lax.broadcasted_iota(jnp.int32, (EXPERTS, TOK), 0)
    chosen = routes_t[0:1, :] == expert
    for k in range(1, 8):
        chosen = chosen | (routes_t[k : k + 1, :] == expert)
    sig = jnp.where(chosen, 1.0 / (1.0 + jnp.exp(-logits)), 0.0)
    gates = sig / jnp.sum(sig, axis=0, keepdims=True)
    upper = jnp.where(row <= col, 1.0, 0.0).astype(BF)
    hit = jnp.where(chosen, 1.0, 0.0)
    rank = jnp.dot(hit.astype(BF), upper, preferred_element_type=F32)
    rank = jnp.where(chosen, rank - 1.0, -1.0)

    def tok(x_, z_, c_=c):
        return (c_ * 4 + x_) * 2 + z_

    own = tok(x, zl)
    XG[own, 0:TOK, :] = normed
    for n in range(4):
        XG[own, TOK : TOK + 16, 128 * n : 128 * (n + 1)] = jnp.concatenate(
            [gates[8 * n : 8 * n + 8], rank[8 * n : 8 * n + 8]], axis=0
        ).astype(BF)
    cp.start(XG.at[own], XG.at[own], t_zl, beside)
    for i in range(2):
        cp.start(XG.at[own], XG.at[own], t_x[0][i], sides[i])
    cp.start(XG.at[own], XG.at[own], t_p[0][0], partner)
    piece = XG.at[tok(x, 1 - zl)]
    cp.arrived(piece, t_zl)
    for i in range(2):
        cp.start(piece, piece, t_x[1][i], sides[i])
    cp.start(piece, piece, t_p[1][0], partner)
    w_forward(0)
    cuts = ((0, 64), (64, ROWS - 64))
    for r in range(2):
        z_ = zl if r == 0 else 1 - zl
        for i in range(2):
            slot = tok(up(x, 3) if i == 0 else up(x), z_)
            cp.arrived(XG.at[slot], t_x[r][i])
            half = XG.at[slot, pl.ds(*cuts[i])]
            cp.start(half, half, t_half[r][i], sides[i])
            cp.start(XG.at[slot], XG.at[slot], t_p[r][1 + i], partner)
    w_forward(1)
    for r in range(2):
        z_ = zl if r == 0 else 1 - zl
        slot = tok(far, z_)
        for i in range(2):
            cp.arrived(XG.at[slot, pl.ds(*cuts[i])], t_half[r][i])
        cp.start(XG.at[slot], XG.at[slot], t_p[r][3], partner)
    w_forward(2)
    for r in range(2):
        z_ = zl if r == 0 else 1 - zl
        for i, from_x in enumerate((x, up(x, 3), up(x), far)):
            cp.arrived(XG.at[tok(from_x, z_, 1 - c)], t_p[r][i])
    for n in range(3):
        w_finish(n)

    e_cols = pl.ds(pl.multiple_of(x * 128, 128), 128)
    slot_row = lax.broadcasted_iota(jnp.int32, (TOK, TOK), 0)
    slot_f = jnp.where(slot_row < CAP, slot_row, slot_row - CAP).astype(F32)
    first = slot_row < CAP
    sub = lax.broadcasted_iota(jnp.int32, (8, TOK), 0)
    picks = [sub == (2 * zl + j) * 2 + c for j in range(2)]
    sources = [(rel_c, rel_z) for rel_c in range(2) for rel_z in range(2)]
    Y[...] = jnp.zeros_like(Y)

    first_c = cp.sends
    cp.sends += 8

    def chunk_copy(n):
        return pltpu.make_async_remote_copy(
            src_ref=CS.at[n],
            dst_ref=CR.at[n],
            send_sem=send_sem.at[first_c + n],
            recv_sem=recv_sem.at[s_c + n],
            device_id=partner,
            device_id_type=MESH,
        )

    def chunk(n):
        from_x = lax.rem(x + 2 - n + 3 * lax.div(n, 2) - 2 * lax.div(n, 3), 4)
        for s, (rel_c, rel_z) in enumerate(sources):
            slot = tok(from_x, lax.rem(zl + rel_z, 2), lax.rem(c + rel_c, 2))
            info = XG[slot, TOK : TOK + 16, e_cols].astype(F32)
            gate, rank = [
                [jnp.sum(jnp.where(pick, part, 0.0), axis=0, keepdims=True) for pick in picks]
                for part in (info[0:8], info[8:16])
            ]
            here = jnp.where(first, rank[0], rank[1]) == slot_f
            table = jnp.where(here, 1.0, 0.0).astype(BF)
            CM[s] = jnp.where(here, jnp.where(first, gate[0], gate[1]), 0.0).T.astype(BF)
            rows = jnp.dot(table, XG[slot, 0:TOK, :], preferred_element_type=F32).astype(BF)
            XD[0, s * CAP : (s + 1) * CAP, :] = rows[0:CAP]
            XD[1, s * CAP : (s + 1) * CAP, :] = rows[CAP : 2 * CAP]
        for j in range(2):
            gu = jnp.dot(XD[j], W1[j].reshape(D, 2 * FFE), preferred_element_type=F32)
            g, u = gu[:, :FFE], gu[:, FFE:]
            act = (g / (1.0 + jnp.exp(-g)) * u).astype(BF)
            res = jnp.dot(act, W2[j].reshape(FFE, D), preferred_element_type=F32).astype(BF)
            for s in range(4):
                Y[s, j * CAP : (j + 1) * CAP, :] = res[s * CAP : (s + 1) * CAP]
        for s, (rel_c, rel_z) in enumerate(sources):
            part = jnp.dot(CM[s], Y[s], preferred_element_type=F32)
            if rel_c == 0:
                PF[n * 2 + rel_z] = part
            else:
                CS[n * 2 + rel_z] = part.astype(BF)
                chunk_copy(n * 2 + rel_z).start()

    def summed(n, r):
        cp.arrived(CR.at[2 * n + r], s_c + 2 * n + r)
        return PF[2 * n + r] + CR[2 * n + r].astype(F32)

    def reduce_far():
        for r in range(2):
            S1S[r] = summed(0, r).astype(BF)
            for i in range(2):
                cut = pl.ds(64 * i, 64)
                cp.start(
                    S1S.at[r, cut],
                    S1R.at[r, cut],
                    s_1[r][i],
                    sides[i],
                    functools.partial(lambda r, i: S1S.at[r, pl.ds(64 * i, 64)], r, i),
                )

    def reduce_side(i):
        for r in range(2):
            part = summed(1 + i, r)
            cut = pl.ds(64 * i, 64)
            cp.arrived(S1R.at[r, cut], s_1[r][i])
            S2S[i, r] = part.astype(BF)
            S2S[i, r, cut, :] = (part[64 * i : 64 * i + 64] + S1R[r, cut, :].astype(F32)).astype(BF)
            cp.start(
                S2S.at[i, r],
                S2R.at[i, r],
                s_2[i][r],
                sides[i],
                functools.partial(lambda i, r: S2S.at[i, r], i, r),
            )

    @pl.loop(0, 4)
    def _(n):
        chunk(n)

        @pl.when(n == 1)
        def _():
            reduce_far()

        @pl.when(n == 2)
        def _():
            reduce_side(0)

        @pl.when(n == 3)
        def _():
            reduce_side(1)

    for r in (1, 0):
        part = summed(3, r)
        for i in range(2):
            cp.arrived(S2R.at[i, r], s_2[i][r])
            part += S2R[i, r].astype(F32)
        if r == 1:
            ZS[...] = part.astype(BF)
            cp.start(ZS, ZR, s_z, beside)
    cp.arrived(ZR, s_z)
    out[...] = (HID[...] + part + ZR[...].astype(F32)).astype(BF)

    for n in range(8):
        chunk_copy(n).wait_send()
    w_drain()
    cp.drain()


def per_device(
    resid, queries, suffix_kv, prefix_kv, segments, o_weight, norm_gain, router, routes, w_gate_up, w_down
):
    vm = pl.BlockSpec(memory_space=pltpu.VMEM)
    hbm = pl.BlockSpec(memory_space=pl.ANY)
    args = (
        resid,
        queries,
        suffix_kv.reshape(TOK, 1024),
        prefix_kv.reshape(64, 1024),
        segments,
        segments.reshape(TOK, 1),
        jnp.pad(o_weight, ((0, 2), (0, 0))),
        jnp.asarray(spread_matrix(), BF),
        norm_gain.reshape(1, D),
        router.T,
        routes.T,
        w_gate_up.reshape(2, 96, 1024),
        w_down.reshape(64, D),
    )
    specs = [vm, vm, vm, hbm, vm, vm, hbm, vm, vm, vm, vm, hbm, hbm]
    return pl.pallas_call(
        kernel,
        out_shape=jax.ShapeDtypeStruct((TOK, D), BF),
        in_specs=specs,
        out_specs=vm,
        scratch_shapes=[
            pltpu.VMEM((32, 64, 1024), BF),
            pltpu.VMEM((4, 2, 4, 8, 8, D), BF),
            pltpu.VMEM((2, 4, 2, 2, 96, 1024), BF),
            pltpu.VMEM((2, 4, 2, 64, D), BF),
            pltpu.VMEM((16, ROWS, D), BF),
            pltpu.VMEM((8, 384, 128), BF),
            pltpu.VMEM((8, 384, 128), F32),
            pltpu.VMEM((4, TOK, 512), BF),
            pltpu.VMEM((384, TOK), F32),
            pltpu.VMEM((TOK, D), F32),
            pltpu.VMEM((2, 4 * CAP, D), BF),
            pltpu.VMEM((4, TOK, D), BF),
            pltpu.VMEM((4, TOK, TOK), BF),
            pltpu.VMEM((8, TOK, D), F32),
            pltpu.VMEM((8, TOK, D), BF),
            pltpu.VMEM((8, TOK, D), BF),
            pltpu.VMEM((2, TOK, D), BF),
            pltpu.VMEM((2, TOK, D), BF),
            pltpu.VMEM((2, 2, TOK, D), BF),
            pltpu.VMEM((2, 2, TOK, D), BF),
            pltpu.VMEM((TOK, D), BF),
            pltpu.VMEM((TOK, D), BF),
            pltpu.SemaphoreType.DMA((192,)),
            pltpu.SemaphoreType.DMA((192,)),
            pltpu.SemaphoreType.DMA((2,)),
        ],
        compiler_params=pltpu.CompilerParams(
            collective_id=0, has_side_effects=True, vmem_limit_bytes=67043328
        ),
    )(*args)


def solution(mesh):
    return jax.shard_map(
        per_device,
        mesh=mesh,
        in_specs=(
            P(("grp", "dev"), None),
            P(("grp", "dev"), None),
            P(("grp", "dev"), None, None),
            P("grp", "dev", None, None),
            P(("grp", "dev"), None),
            P(("grp", "dev"), None),
            P(),
            P(),
            P(("grp", "dev"), None),
            P("dev", "grp", None),
            P("dev", "grp", None),
        ),
        out_specs=P(("grp", "dev"), None),
        check_vma=False,
    )
```

time: 976 us -> 216 us (0.22)
  waiting for transfers between devices: 693 us -> 0 us
  Pallas kernels: 0 us -> 209 us
  local copies, waits for them, and re-layouts: 124 us -> 7.19 us
  other arithmetic: 63.1 us -> 0 us
  matrix products: 50.7 us -> 0 us
  starting transfers between devices: 24.3 us -> 0 us
  between operations: 15.1 us -> 0.02 us
    all_gather x4 -> x0, waiting for transfers between devices: 588 us -> none  [the longest x1 352 us: per_device(): lax.all_gather(o_weight, ('grp', 'dev'), axis=0, tiled=True)]
    pallas_call x0 -> x1, Pallas kernels: none -> 209 us  [per_device(): pl.pallas_call(kernel, out_shape=jax.ShapeDtypeStruct((TOK, D), BF), in_s...]
    all_to_all x2 -> x0, waiting for transfers between devices: 103 us -> none  [the longest x1 103 us: per_device(): lax.all_to_all(expert_out, 'dev', split_axis=1, concat_axis=0, tiled=True)]
    convert_element_type x2 -> x0, local copies, waits for them, and re-layouts: 52.3 us -> none  [the longest x1 52.2 us: per_device(): expert_out = jnp.einsum('erf,efd->erd', sliced, lax.all_gather(w_down, 'g...]
    dot_general x10 -> x0, matrix products: 50.7 us -> none  [the longest x2 11.7 us: update(): jnp.einsum('tgrd,ngd->grtn', query_heads, keys.reshape(count, KVH, HDIM),...]
    unnamed x20 -> x9, local copies, waits for them, and re-layouts: 39.3 us -> 3.87 us
    unnamed x1 -> x0, other arithmetic: 32 us -> none
    slice x8 -> x0, local copies, waits for them, and re-layouts: 31.6 us -> none  [the longest x3 29.5 us: per_device(): carry = update(initial, piece[:, 0], piece[:, 1], None)]
  transfers between devices with their start and end apart: 6 -> 0, of which waited for: 5 -> 0; matrix products, arithmetic and copies ran while one was open for 10% -> 0% of each run, Pallas kernels for 0% -> 0%
where the time goes in v1:
time: 216 us
  Pallas kernels  209 us (97%)
  local copies, waits for them, and re-layouts  7.19 us (3%)
    pallas_call x1, Pallas kernels, per_device(): pl.pallas_call(kernel, out_shape=jax.ShapeDtypeStruct((TOK, D), BF), in_s...  209 us

profile of v1, /device:TPU:70, one launch (start us, length us, event | category | flops | bytes accessed | tf_op | source)
XLA Modules:
  0.0 216.2 jit_solution(5545046994367076559)
XLA Ops:
  0.0 0.0 copy-start.2
  0.0 0.0 copy-start.1
  0.0 0.0 copy-start
  0.0 0.7 copy-done.2
  0.7 0.6 reshape.21.gain
  1.3 1.3 pad.4.o_own
  2.6 1.4 copy.13.seg_col
  4.0 0.0 copy-done.1
  4.0 0.7 copy.15
  4.7 0.0 copy-done
  4.7 0.7 copy.14
  5.4 209.0 %shard_map.118 = bf16[128,1536]{1,0:T(8,128)(2,1)} custom-call(bf16[128,1536]{1,0:T(8,128)(2,1)} %resid.1, bf16[128,1536]{1,0:T(8,128)(2,1)} %queries.1, bf16[128,1024]{1,0:T(8,128)(2,1)} %bitcast.10, bf16[64,1024]{1,0:T(8,128)(2,1)} %bitcast.11, s32[1,128]{1,0:T(1,128)} %seg_row.1, s32[128,1]{1,0:T(8,128)} %copy.13.seg_col, bf16[8,1536]{1,0:T(8,128)(2,1)} %pad.4.o_own, ...), custom_call_target="tpu_custom_call" | custom-call | tf_op jit(solution)/shard_map/pallas_call | solution.py:571
  214.5 1.8 copy.17
Async XLA Ops:
  0.0 0.7 copy-start.2
  0.0 4.0 %copy-start.1 = (bf16[1,64,2,512]{3,2,1,0:T(2,128)(2,1)S(1)}, bf16[1,64,2,512]{3,2,1,0:T(2,128)(2,1)}, u32[]{:S(2)}) copy-start(bf16[1,64,2,512]{3,2,1,0:T(2,128)(2,1)} %param.15) | copy-start | bytes 393220
  0.0 4.7 %copy-start = (bf16[128,2,512]{2,1,0:T(2,128)(2,1)S(1)}, bf16[128,2,512]{2,1,0:T(2,128)(2,1)}, u32[]{:S(2)}) copy-start(bf16[128,2,512]{2,1,0:T(2,128)(2,1)} %param.14) | copy-start | bytes 786436

commit v2 on v1

--- a/solution.py
+++ b/solution.py
@@ -298,6 +298,7 @@
                 cp.arrived(O.at[y, c, x, zz], o_z[k][j])
     for k in (1, 2, 3):
         cp.start(O.at[y, c, x], O.at[y, c, x], o_y[k], at(y_=up(y, k)))
+    w_along_y(0)
     for k in range(4):
         slot = kv_slot(up(x, 2), up(zh, 4 - k))
         for i in range(2):
@@ -308,6 +309,7 @@
     for i in range(2):
         cp.start(O.at[:, c, x], O.at[:, c, x], o_x[i], sides[i])
     cp.start(O.at[:, c, x], O.at[:, c, x], o_p[0], partner)
+    w_along_y(1)
     for k in range(4):
         for i, from_x in enumerate((x, up(x, 3), up(x), up(x, 2))):
             cp.arrived(KV.at[kv_slot(from_x, up(zh, 4 - k), 1 - c)], kv_p[k][i])
@@ -329,17 +331,10 @@
         acc += jnp.dot(p2.astype(BF), suffix[:, v_cols], preferred_element_type=F32)
         OH[h] = acc / total
 
-    @pl.loop(0, 2)
+    @pl.loop(0, 4)
     def _(h):
         attend(h)
 
-    w_along_y(0)
-
-    @pl.loop(2, 5)
-    def _(h):
-        attend(h)
-
-    w_along_y(1)
     for i in range(2):
         origin = up(x, 3) if i == 0 else up(x)
         cp.arrived(O.at[:, c, origin], o_x[i])
@@ -347,9 +342,13 @@
         cp.start(half, half, o_half[i], sides[i])
         cp.start(O.at[:, c, origin], O.at[:, c, origin], o_p[1 + i], partner)
 
-    @pl.loop(5, 8)
+    w_along_y(2)
+
+    @pl.loop(4, 8)
     def _(h):
         attend(h)
+
+    w_forward(0)
 
     for p in range(4):
         a = [OH[2 * p + h // 3, (h % 3) * 128 : (h % 3 + 1) * 128, :] for h in range(6)]
@@ -365,7 +364,6 @@
     for i in range(2):
         cp.arrived(O.at[pl.ds(2 * i, 2), c, far], o_half[i])
     cp.start(O.at[:, c, far], O.at[:, c, far], o_p[3], partner)
-    w_along_y(2)
     for i, from_x in enumerate((x, up(x, 3), up(x), far)):
         cp.arrived(O.at[:, 1 - c, from_x], o_p[i])
 
@@ -405,7 +403,7 @@
     for i in range(2):
         cp.start(piece, piece, t_x[1][i], sides[i])
     cp.start(piece, piece, t_p[1][0], partner)
-    w_forward(0)
+    w_forward(1)
     cuts = ((0, 64), (64, ROWS - 64))
     for r in range(2):
         z_ = zl if r == 0 else 1 - zl
@@ -415,14 +413,13 @@
             half = XG.at[slot, pl.ds(*cuts[i])]
             cp.start(half, half, t_half[r][i], sides[i])
             cp.start(XG.at[slot], XG.at[slot], t_p[r][1 + i], partner)
-    w_forward(1)
+    w_forward(2)
     for r in range(2):
         z_ = zl if r == 0 else 1 - zl
         slot = tok(far, z_)
         for i in range(2):
             cp.arrived(XG.at[slot, pl.ds(*cuts[i])], t_half[r][i])
         cp.start(XG.at[slot], XG.at[slot], t_p[r][3], partner)
-    w_forward(2)
     for r in range(2):
         z_ = zl if r == 0 else 1 - zl
         for i, from_x in enumerate((x, up(x, 3), up(x), far)):
@@ -487,7 +484,7 @@
         return PF[2 * n + r] + CR[2 * n + r].astype(F32)
 
     def reduce_far():
-        for r in range(2):
+        for r in (1, 0):
             S1S[r] = summed(0, r).astype(BF)
             for i in range(2):
                 cut = pl.ds(64 * i, 64)
@@ -500,7 +497,7 @@
                 )
 
     def reduce_side(i):
-        for r in range(2):
+        for r in (1, 0):
             part = summed(1 + i, r)
             cut = pl.ds(64 * i, 64)
             cp.arrived(S1R.at[r, cut], s_1[r][i])

time: 216 us -> 213 us (0.986)
  Pallas kernels: 209 us -> 206 us
    pallas_call x1, Pallas kernels: 209 us -> 206 us  [per_device(): pl.pallas_call(kernel, out_shape=jax.ShapeDtypeStruct((TOK, D), BF), in_s...]
where the time goes in v2:
time: 213 us
  Pallas kernels  206 us (97%)
  local copies, waits for them, and re-layouts  7.19 us (3%)
    pallas_call x1, Pallas kernels, per_device(): pl.pallas_call(kernel, out_shape=jax.ShapeDtypeStruct((TOK, D), BF), in_s...  206 us

profile of v2, /device:TPU:70, one launch (start us, length us, event | category | flops | bytes accessed | tf_op | source)
XLA Modules:
  0.0 213.1 jit_solution(17090986758091552071)
XLA Ops:
  0.0 0.0 copy-start.2
  0.0 0.0 copy-start.1
  0.0 0.0 copy-start
  0.0 0.7 copy-done.2
  0.7 0.6 reshape.21.gain
  1.3 1.3 pad.4.o_own
  2.6 1.4 copy.13.seg_col
  4.0 0.0 copy-done.1
  4.0 0.7 copy.15
  4.7 0.0 copy-done
  4.7 0.7 copy.14
  5.4 205.9 %shard_map.118 = bf16[128,1536]{1,0:T(8,128)(2,1)} custom-call(bf16[128,1536]{1,0:T(8,128)(2,1)} %resid.1, bf16[128,1536]{1,0:T(8,128)(2,1)} %queries.1, bf16[128,1024]{1,0:T(8,128)(2,1)} %bitcast.10, bf16[64,1024]{1,0:T(8,128)(2,1)} %bitcast.11, s32[1,128]{1,0:T(1,128)} %seg_row.1, s32[128,1]{1,0:T(8,128)} %copy.13.seg_col, bf16[8,1536]{1,0:T(8,128)(2,1)} %pad.4.o_own, ...), custom_call_target="tpu_custom_call" | custom-call | tf_op jit(solution)/shard_map/pallas_call | solution.py:568
  211.4 1.8 copy.17
Async XLA Ops:
  0.0 0.7 copy-start.2
  0.0 4.0 %copy-start.1 = (bf16[1,64,2,512]{3,2,1,0:T(2,128)(2,1)S(1)}, bf16[1,64,2,512]{3,2,1,0:T(2,128)(2,1)}, u32[]{:S(2)}) copy-start(bf16[1,64,2,512]{3,2,1,0:T(2,128)(2,1)} %param.15) | copy-start | bytes 393220
  0.0 4.7 %copy-start = (bf16[128,2,512]{2,1,0:T(2,128)(2,1)S(1)}, bf16[128,2,512]{2,1,0:T(2,128)(2,1)}, u32[]{:S(2)}) copy-start(bf16[128,2,512]{2,1,0:T(2,128)(2,1)} %param.14) | copy-start | bytes 786436

commit v3 on v2

--- a/solution.py
+++ b/solution.py
@@ -65,12 +65,11 @@
     suffix,
     kv_own,
     seg_row,
-    seg_col,
     o_own,
     spread,
     gain,
     router_t,
-    routes_t,
+    routes,
     w1_own,
     w2_own,
     out,
@@ -271,7 +270,8 @@
             QH[2 * p + h // 3, (h % 3) * 128 : (h % 3 + 1) * 128, :] = heads[h].astype(BF)
     row = lax.broadcasted_iota(jnp.int32, (TOK, TOK), 0)
     col = lax.broadcasted_iota(jnp.int32, (TOK, TOK), 1)
-    allowed = (seg_row[...] == seg_col[...]) & (col <= row)
+    seg = jnp.broadcast_to(seg_row[...].astype(F32), (TOK, TOK))
+    allowed = (seg == seg.T) & (col <= row)
     bias = jnp.where(allowed, 0.0, -1e30)
     for i in range(3):
         MK[i * 128 : (i + 1) * 128, :] = bias
@@ -374,7 +374,8 @@
     scale = lax.rsqrt(jnp.mean(total * total, axis=1, keepdims=True) + 1e-06)
     normed = (total * scale * gain[...]).astype(BF)
     logits = lax.dot_general(router_t[...], normed, nt, preferred_element_type=F32)
-    expert = lax.broadcasted_iota(jnp.int32, (EXPERTS, TOK), 0)
+    routes_t = routes[...].astype(F32).T
+    expert = lax.broadcasted_iota(jnp.int32, (EXPERTS, TOK), 0).astype(F32)
     chosen = routes_t[0:1, :] == expert
     for k in range(1, 8):
         chosen = chosen | (routes_t[k : k + 1, :] == expert)
@@ -555,16 +556,15 @@
         suffix_kv.reshape(TOK, 1024),
         prefix_kv.reshape(64, 1024),
         segments,
-        segments.reshape(TOK, 1),
         jnp.pad(o_weight, ((0, 2), (0, 0))),
         jnp.asarray(spread_matrix(), BF),
         norm_gain.reshape(1, D),
         router.T,
-        routes.T,
+        routes,
         w_gate_up.reshape(2, 96, 1024),
         w_down.reshape(64, D),
     )
-    specs = [vm, vm, vm, hbm, vm, vm, hbm, vm, vm, vm, vm, hbm, hbm]
+    specs = [vm, vm, vm, hbm, vm, hbm, vm, vm, vm, vm, hbm, hbm]
     return pl.pallas_call(
         kernel,
         out_shape=jax.ShapeDtypeStruct((TOK, D), BF),

time: 213 us -> 213 us (level)
    unnamed x9 -> x10, local copies, waits for them, and re-layouts: 3.87 us -> 5.28 us
where the time goes in v3:
time: 213 us
  Pallas kernels  206 us (97%)
  local copies, waits for them, and re-layouts  7.22 us (3%)
    pallas_call x1, Pallas kernels, per_device(): pl.pallas_call(kernel, out_shape=jax.ShapeDtypeStruct((TOK, D), BF), in_s...  206 us
    unnamed x10, local copies, waits for them, and re-layouts  5.28 us

profile of v3, /device:TPU:70, one launch (start us, length us, event | category | flops | bytes accessed | tf_op | source)
XLA Modules:
  0.0 213.2 jit_solution(9583963405410250092)
XLA Ops:
  0.0 0.0 copy-start.2
  0.0 0.0 copy-start.1
  0.0 0.0 copy-start
  0.0 0.7 copy-done.2
  0.7 0.6 reshape.17.gain
  1.3 1.3 pad.4.o_own
  2.6 1.4 copy.13.routes
  4.0 0.0 copy-done.1
  4.0 0.7 copy.15
  4.7 0.0 copy-done
  4.7 0.7 copy.14
  5.5 205.9 %shard_map.118 = bf16[128,1536]{1,0:T(8,128)(2,1)} custom-call(bf16[128,1536]{1,0:T(8,128)(2,1)} %resid.1, bf16[128,1536]{1,0:T(8,128)(2,1)} %queries.1, bf16[128,1024]{1,0:T(8,128)(2,1)} %bitcast.8, bf16[64,1024]{1,0:T(8,128)(2,1)} %bitcast.9, s32[1,128]{1,0:T(1,128)} %seg_row.1, bf16[8,1536]{1,0:T(8,128)(2,1)} %pad.4.o_own, ...), custom_call_target="tpu_custom_call" | custom-call | tf_op jit(solution)/shard_map/pallas_call | solution.py:568
  211.4 1.8 copy.17
Async XLA Ops:
  0.0 0.7 copy-start.2
  0.0 4.0 %copy-start.1 = (bf16[1,64,2,512]{3,2,1,0:T(2,128)(2,1)S(1)}, bf16[1,64,2,512]{3,2,1,0:T(2,128)(2,1)}, u32[]{:S(2)}) copy-start(bf16[1,64,2,512]{3,2,1,0:T(2,128)(2,1)} %param.15) | copy-start | bytes 393220
  0.0 4.7 %copy-start = (bf16[128,2,512]{2,1,0:T(2,128)(2,1)S(1)}, bf16[128,2,512]{2,1,0:T(2,128)(2,1)}, u32[]{:S(2)}) copy-start(bf16[128,2,512]{2,1,0:T(2,128)(2,1)} %param.14) | copy-start | bytes 786436
